TPU v7x, 32 devices: a whole 2x2x4 slice. The times are simulated.
32 devices in a mesh: sample: 2 (over core), sx: 4 (over y, x), sy: 4 (over z).
Axes of the slice: x: 2, y: 2, z: 4, core: 2. Of those that a mesh axis runs over, the one named last changes fastest.
Arguments:
- features: bfloat16 [16, 4, 16, 32, 256], P('sx', 'sample', 'sy'), may hold values from -6 to 6
- kernel: bfloat16 [3, 3, 3, 256, 256], P(None, None, None, 'sx', 'sy'), may hold values from -0.078125 to 0.078125
- filter_bias: bfloat16 [256], P('sy'), may hold values from -3 to 3
- cotangent: bfloat16 [16, 4, 16, 32, 256], P('sx', 'sample', None, None, 'sy'), may hold values from -6 to 6
Outputs:
- output: bfloat16 [16, 4, 16, 32, 256], P('sx', 'sample', None, None, 'sy')
- input_grad: bfloat16 [16, 4, 16, 32, 256], P('sx', 'sample', 'sy')
- kernel_grad: float32 [3, 3, 3, 256, 256], P(None, None, None, 'sx', 'sy')
All inputs are finite; a program needn't handle non-finite values.
Results may differ from a plain program's by a relative error of at most 0.014.
Values may be sent and summed in bfloat16 or wider, within the bound.
A program may use at most 128 MiB of HBM per device.

v0:
```python
import jax
import jax.numpy as jnp
from jax import lax
from jax.sharding import PartitionSpec as P


def padded_2(array, sides, width):
    for axis, dim in sides:
        size, length = (lax.axis_size(axis), array.shape[dim])
        up = [(i, (i + 1) % size) for i in range(size - 1)]
        down = [(j, i) for i, j in up]
        last = lax.slice_in_dim(array, length - width, length, axis=dim)
        leading = lax.slice_in_dim(array, 0, width, axis=dim)
        before = lax.ppermute(last, axis, up)
        after = lax.ppermute(leading, axis, down)
        array = jnp.concatenate([before, array, after], axis=dim)
    return array


def slope_of(hidden):
    gate = jax.nn.sigmoid(hidden)
    return gate * (1.0 + hidden * (1.0 - gate))


def convolve(inputs, weights, pads, layout):
    return lax.conv_general_dilated(
        inputs,
        weights,
        (1, 1, 1),
        pads,
        dimension_numbers=layout,
        preferred_element_type=jnp.float32,
    )


def forward_conv(inputs, weights):
    return convolve(inputs, weights, ((0, 0), (0, 0), (0, 0)), ("DNHWC", "DHWIO", "DNHWC"))


def kernel_grad_of(window, grad_pre):
    return convolve(window, grad_pre, ((0, 0), (0, 0), (0, 0)), ("DCHWN", "DIHWO", "DHWNC"))


def local(features, kernel, filter_bias, cotangent):
    kernel_full = lax.all_gather(kernel, "sx", axis=3, tiled=True)
    edged = padded_2(features, (("sx", 0),), 1)
    band = lax.all_gather(edged, "sy", axis=2, tiled=True)
    padded = jnp.pad(band, ((0, 0), (0, 0), (1, 1), (1, 1), (0, 0)))
    hidden = forward_conv(padded, kernel_full) + filter_bias.astype(jnp.float32)
    output = jax.nn.silu(hidden).astype(jnp.bfloat16)
    grad_pre = (cotangent.astype(jnp.float32) * slope_of(hidden)).astype(jnp.bfloat16)
    grad_band = padded_2(grad_pre, (("sx", 0),), 1)
    grad_padded = jnp.pad(grad_band, ((0, 0), (0, 0), (1, 1), (1, 1), (0, 0)))
    flipped = kernel_full[::-1, ::-1, ::-1]
    partial_grad = convolve(
        grad_padded, flipped, ((0, 0), (0, 0), (0, 0)), ("DNHWC", "DHWOI", "DNHWC")
    )
    input_grad = lax.psum_scatter(
        partial_grad.astype(jnp.bfloat16), "sy", scatter_dimension=2, tiled=True
    )
    local_grad = kernel_grad_of(padded, grad_pre)
    weight_sum = lax.psum_scatter(
        local_grad.astype(jnp.bfloat16), "sx", scatter_dimension=3, tiled=True
    )
    kernel_grad = lax.psum(weight_sum, "sample").astype(jnp.float32)
    return (output, input_grad, kernel_grad)


def solution(mesh):
    return jax.shard_map(
        local,
        mesh=mesh,
        in_specs=(
            P("sx", "sample", "sy", None, None),
            P(None, None, None, "sx", "sy"),
            P("sy"),
            P("sx", "sample", None, None, "sy"),
        ),
        out_specs=(
            P("sx", "sample", None, None, "sy"),
            P("sx", "sample", "sy", None, None),
            P(None, None, None, "sx", "sy"),
        ),
        check_vma=False,
    )
```

profile of v0, /device:TPU:0, one launch (start us, length us, event | category | flops | bytes accessed | tf_op | source)
XLA Modules:
  0.0 269.2 jit_solution(10570267025638348491)
XLA Ops:
  7.2 1.6 copy.28
  9.1 4.9 %collective-permute-start = (bf16[1,2,4,32,256]{4,1,3,2,0:T(2,128)(2,1)S(1)}, bf16[1,2,4,32,256]{4,1,3,2,0:T(2,128)(2,1)S(1)}, u32[]{:S(2)}, u32[]{:S(2)}) collective-permute-start(bf16[1,2,4,32,256]{4,1,3,2,0:T(2,128)(2,1)S(1)} %get-tuple-element.13), channel_id=1, source_target_pairs={{0,4},{4,8},{8,12},{1,5},{5,9},{9,13},{2,6},{6,10},{10,14},{3,7},{... | collective-permute-start | bytes 393224 | tf_op jit(solution)/shard_map/ppermute | solution.py:14
  13.9 1.3 collective-permute-start.1
  15.2 1.4 collective-permute-done
  16.7 4.8 %collective-permute-done.1 = bf16[1,2,4,32,256]{4,1,3,2,0:T(2,128)(2,1)S(1)} collective-permute-done((bf16[1,2,4,32,256]{4,1,3,2,0:T(2,128)(2,1)S(1)}, bf16[1,2,4,32,256]{4,1,3,2,0:T(2,128)(2,1)S(1)}, u32[]{:S(2)}, u32[]{:S(2)}) %collective-permute-start.1) | collective-permute-done | bytes 131104 | tf_op jit(solution)/shard_map/ppermute | solution.py:15
  21.4 2.1 pad_maximum_fusion
  23.6 17.6 %all_gather.7 = bf16[3,3,3,256,64]{4,3,2,1,0:T(8,128)(2,1)S(1)} all-gather(bf16[3,3,3,64,64]{4,3,2,1,0:T(8,128)(2,1)S(1)} %copy-done.5), channel_id=1, replica_groups=mesh['sample'=2,'sx'=4,'sy'=4] {'sx'}, dimensions={3}, use_global_device_ids=true | all-gather | bytes 1105920 | tf_op jit(solution)/shard_map/all_gather | solution.py:45
  41.2 46.4 %all-gather.2.cloned.1.call-done = bf16[6,2,16,32,256]{4,1,3,2,0:T(2,128)(2,1)} async-done(((bf16[6,2,4,32,256]{4,1,3,2,0:T(2,128)(2,1)}), bf16[6,2,16,32,256]{4,1,3,2,0:T(2,128)(2,1)}) %all-gather.2.cloned.1.call-update) | async-done | bytes 3145744 | tf_op jit(solution)/shard_map/all_gather | solution.py:47
  87.7 4.8 %pad.4 = bf16[6,16,2,40,256]{4,2,3,1,0:T(2,128)(2,1)S(1)} pad(bf16[6,16,2,32,256]{4,2,3,1,0:T(2,128)(2,1)} %bitcast.37, bf16[]{:T(256)} %constant.6), padding=0_0x0_0x0_0x1_7x0_0 | pad | bytes 7077890 | tf_op jit(solution)/shard_map/all_gather | solution.py:47
  94.0 21.8 %add_multiply_fusion = (f32[4,16,16,5,64]{4,2,3,1,0:T(8,128)S(1)}, bf16[4,16,16,5,64]{4,2,3,1,0:T(8,128)(2,1)}) fusion(f32[64]{0:T(128)S(1)} %convert_element_type.25, pred[16,5]{0,1:T(8,128)(4,1)S(1)} %copy-done.7, bf16[3,3,3,256,64]{4,3,2,1,0:T(8,128)(2,1)S(1)} %all_gather.7, bf16[6,16,2,7,2,256]{5,3,2,4,1,0:T(8,128)(2,1)S(1)} %slice.23, ...), kind=kOutput, calls=%fused_computation.16 | convolution fusion | flops 4361224192 | bytes 8159568 | tf_op jit(solution)/shard_map/conv_general_dilated | solution.py:26
  117.6 0.8 fusion.22
  118.4 4.1 %collective-permute-start.2 = (bf16[1,2,16,32,64]{4,2,3,1,0:T(8,128)(2,1)}, bf16[1,2,16,32,64]{4,2,3,1,0:T(8,128)(2,1)}, u32[]{:S(2)}, u32[]{:S(2)}) collective-permute-start(bf16[1,2,16,32,64]{4,2,3,1,0:T(8,128)(2,1)} %get-tuple-element.11), channel_id=1, source_target_pairs={{0,4},{4,8},{8,12},{1,5},{5,9},{9,13},{2,6},{6,10},{10,14},{3,7},{... | collective-permute-start | bytes 393224 | tf_op jit(solution)/shard_map/ppermute | solution.py:14
  122.5 1.3 collective-permute-start.3
  123.8 36.4 %convolution_convert_fusion = bf16[3,3,3,256,64]{4,3,2,1,0:T(8,128)(2,1)} fusion(bf16[6,2,16,32,256]{4,1,3,2,0:T(2,128)(2,1)S(1)} %copy-done, bf16[4,2,16,32,64]{4,2,3,1,0:T(8,128)(2,1)S(1)} %fusion.15), kind=kOutput, calls=%fused_computation.24 | convolution fusion | flops 3400974336 | bytes 4554752 | tf_op jit(solution)/shard_map/conv_general_dilated | solution.py:26
  160.3 1.4 maximum_bitcast_fusion
  163.8 10.1 %select_convert_fusion = bf16[4,16,16,5,256]{4,2,3,1,0:T(8,128)(2,1)S(1)} fusion(pred[16,5]{0,1:T(8,128)(4,1)S(1)} %copy-done.8, bf16[3,3,3,256,64]{4,3,2,1,0:T(8,128)(2,1)S(1)} %copy-done.2, bf16[6,16,2,8,7,64]{5,1,4,3,2,0:T(8,128)(2,1)S(1)} %fusion.9), kind=kOutput, calls=%fused_computation.10 | convolution fusion | flops 4343726080 | bytes 4882512 | tf_op jit(solution)/shard_map/conv_general_dilated | solution.py:26
  173.8 1.0 copy.37
  174.8 17.9 %reduce-scatter.5.cloned.1.call-done = bf16[3,3,3,64,64]{4,3,2,1,0:T(8,128)(2,1)} async-done(((bf16[3,3,3,256,64]{4,3,2,1,0:T(8,128)(2,1)}), bf16[3,3,3,64,64]{4,3,2,1,0:T(8,128)(2,1)}) %reduce-scatter.5.cloned.1.call-update) | async-done | bytes 221200 | tf_op jit(solution)/shard_map/reduce_scatter | solution.py:62
  193.0 2.1 copy.38
  195.6 1.2 copy.40
  196.9 16.7 %all-reduce.2.cloned.1.call-done = bf16[3,3,3,64,64]{4,3,2,1,0:T(8,128)(2,1)} async-done(((bf16[3,3,3,64,64]{4,3,2,1,0:T(8,128)(2,1)}), bf16[3,3,3,64,64]{4,3,2,1,0:T(8,128)(2,1)}) %all-reduce.2.cloned.1.call-update) | async-done | bytes 221200 | tf_op jit(solution)/shard_map/psum | solution.py:65
  213.6 2.0 convert_element_type.31
  215.6 45.0 %reduce-scatter.3.cloned.1.call-done = bf16[4,2,4,32,256]{4,3,1,0,2:T(8,128)(2,1)} async-done(((bf16[4,2,16,32,256]{4,3,1,0,2:T(8,128)(2,1)}), bf16[4,2,4,32,256]{4,3,1,0,2:T(8,128)(2,1)}) %reduce-scatter.3.cloned.1.call-update) | async-done | bytes 524304 | tf_op jit(solution)/shard_map/reduce_scatter | solution.py:58
  260.6 1.9 copy.41
  (40 shorter events, 6.3 us)
Async XLA Ops:
  7.2 16.4 %copy-start.6 = (bf16[64]{0:T(256)(128)(2,1)S(1)}, bf16[64]{0:T(256)(128)(2,1)}, u32[]{:S(2)}) copy-start(bf16[64]{0:T(256)(128)(2,1)} %param.6) | copy-start | bytes 388
  7.2 16.4 %copy-start.5 = (bf16[3,3,3,64,64]{4,3,2,1,0:T(8,128)(2,1)S(1)}, bf16[3,3,3,64,64]{4,3,2,1,0:T(8,128)(2,1)}, u32[]{:S(2)}) copy-start(bf16[3,3,3,64,64]{4,3,2,1,0:T(8,128)(2,1)} %param.5) | copy-start | bytes 663556
  7.2 80.5 %all-gather.2.cloned.1.call-start = ((), (), s32[]{:S(2)}) async-start(), calls=%async_computation.2 | async-start | bytes 3932160 | tf_op jit(solution)/shard_map/all_gather | solution.py:47
  9.1 7.6 %collective-permute-start = (bf16[1,2,4,32,256]{4,1,3,2,0:T(2,128)(2,1)S(1)}, bf16[1,2,4,32,256]{4,1,3,2,0:T(2,128)(2,1)S(1)}, u32[]{:S(2)}, u32[]{:S(2)}) collective-permute-start(bf16[1,2,4,32,256]{4,1,3,2,0:T(2,128)(2,1)S(1)} %get-tuple-element.13), channel_id=1, source_target_pairs={{0,4},{4,8},{8,12},{1,5},{5,9},{9,13},{2,6},{6,10},{10,14},{3,7},{... | collective-permute-start | bytes 393224 | tf_op jit(solution)/shard_map/ppermute | solution.py:14
  13.9 7.5 %collective-permute-start.1 = (bf16[1,2,4,32,256]{4,1,3,2,0:T(2,128)(2,1)S(1)}, bf16[1,2,4,32,256]{4,1,3,2,0:T(2,128)(2,1)S(1)}, u32[]{:S(2)}, u32[]{:S(2)}) collective-permute-start(bf16[1,2,4,32,256]{4,1,3,2,0:T(2,128)(2,1)S(1)} %get-tuple-element.14), channel_id=1, source_target_pairs={{4,0},{8,4},{12,8},{5,1},{9,5},{13,9},{6,2},{10,6},{14,10},{7,3},{... | collective-permute-start | bytes 393224 | tf_op jit(solution)/shard_map/ppermute | solution.py:15
  23.5 169.2 %reduce-scatter.5.cloned.1.call-start = ((), (), s32[]{:S(2)}) async-start(), calls=%async_computation.4 | async-start | bytes 2211840 | tf_op jit(solution)/shard_map/reduce_scatter | solution.py:62
  41.2 52.5 %copy-start.1 = (bf16[3,3,3,256,64]{4,3,2,1,0:T(8,128)(2,1)}, bf16[3,3,3,256,64]{4,3,2,1,0:T(8,128)(2,1)S(1)}, u32[]{:S(2)}) copy-start(bf16[3,3,3,256,64]{4,3,2,1,0:T(8,128)(2,1)S(1)} %all_gather.7) | copy-start | bytes 2654212
  93.3 0.7 copy-start.7
  115.8 1.2 copy-start.4
  117.1 6.7 %copy-start = (bf16[6,2,16,32,256]{4,1,3,2,0:T(2,128)(2,1)S(1)}, bf16[6,2,16,32,256]{4,1,3,2,0:T(2,128)(2,1)}, u32[]{:S(2)}) copy-start(bf16[6,2,16,32,256]{4,1,3,2,0:T(2,128)(2,1)} %all-gather.2.cloned.1.call-done) | copy-start | bytes 9437188
  118.4 41.9 %collective-permute-start.2 = (bf16[1,2,16,32,64]{4,2,3,1,0:T(8,128)(2,1)}, bf16[1,2,16,32,64]{4,2,3,1,0:T(8,128)(2,1)}, u32[]{:S(2)}, u32[]{:S(2)}) collective-permute-start(bf16[1,2,16,32,64]{4,2,3,1,0:T(8,128)(2,1)} %get-tuple-element.11), channel_id=1, source_target_pairs={{0,4},{4,8},{8,12},{1,5},{5,9},{9,13},{2,6},{6,10},{10,14},{3,7},{... | collective-permute-start | bytes 393224 | tf_op jit(solution)/shard_map/ppermute | solution.py:14
  122.5 37.8 %collective-permute-start.3 = (bf16[1,2,16,32,64]{4,2,3,1,0:T(8,128)(2,1)}, bf16[1,2,16,32,64]{4,2,3,1,0:T(8,128)(2,1)}, u32[]{:S(2)}, u32[]{:S(2)}) collective-permute-start(bf16[1,2,16,32,64]{4,2,3,1,0:T(8,128)(2,1)} %get-tuple-element.12), channel_id=1, source_target_pairs={{4,0},{8,4},{12,8},{5,1},{9,5},{13,9},{6,2},{10,6},{14,10},{7,3},{... | collective-permute-start | bytes 393224 | tf_op jit(solution)/shard_map/ppermute | solution.py:15
  160.3 53.3 %all-reduce.2.cloned.1.call-start = ((), (), s32[]{:S(2)}) async-start(), calls=%async_computation.5 | async-start | bytes 884736 | tf_op jit(solution)/shard_map/psum | solution.py:65
  162.3 1.5 copy-start.2
  162.3 1.5 copy-start.8
  192.7 67.9 %reduce-scatter.3.cloned.1.call-start = ((), (), s32[]{:S(2)}) async-start(), calls=%async_computation.3 | async-start | bytes 2621440 | tf_op jit(solution)/shard_map/reduce_scatter | solution.py:58
  193.0 2.1 copy-start.3
Sparse Core Ops, SparseCore 0:
  23.6 63.9 all-gather.1
  160.4 32.2 reduce-scatter.4
  195.0 18.4 all-reduce.1
  215.7 44.8 reduce-scatter.2
where the time goes:
time: 272 us; the launch traced here: 269 us
  waiting for transfers between devices  132 us (49%)
  matrix products  68.3 us (25%)
  local copies, waits for them, and re-layouts  18.4 us (7%)
  blocking collectives  17.6 us (6%)
  between operations  14.2 us (5%)
  starting transfers between devices  11.7 us (4%)
  other arithmetic  6.64 us (2%)
    conv_general_dilated x3, matrix products, convolve(): lax.conv_general_dilated(inputs, weights, (1, 1, 1), pads, dimension_numb...  68.3 us
    all_gather x1, waiting for transfers between devices, local(): band = lax.all_gather(edged, 'sy', axis=2, tiled=True)  46.4 us
    reduce_scatter x1, waiting for transfers between devices, local(): lax.psum_scatter(partial_grad.astype(jnp.bfloat16), 'sy', scatter_dimensi...  45 us
    reduce_scatter x1, waiting for transfers between devices, local(): lax.psum_scatter(local_grad.astype(jnp.bfloat16), 'sx', scatter_dimension...  17.9 us
    all_gather x1, blocking collectives, local(): kernel_full = lax.all_gather(kernel, 'sx', axis=3, tiled=True)  17.6 us
    psum x1, waiting for transfers between devices, local(): kernel_grad = lax.psum(weight_sum, 'sample').astype(jnp.float32)  16.7 us
    ppermute x2, starting transfers between devices, padded_2(): before = lax.ppermute(last, axis, up)  8.97 us
    unnamed x21, local copies, waits for them, and re-layouts  6.24 us
  transfers between devices with their start and end apart: 8, of which 6 were waited for; matrix products, arithmetic and copies ran while one was open for 21% of the time, Pallas kernels for 0%

commit v1 on v0

v1 whole, which is shorter than its diff:
```python
import jax
import jax.numpy as jnp
from jax import lax
from jax.sharding import PartitionSpec as P


def padded(array, axis, dim):
    size, length = lax.axis_size(axis), array.shape[dim]
    up = [(i, i + 1) for i in range(size - 1)]
    down = [(j, i) for i, j in up]
    last = lax.slice_in_dim(array, length - 1, length, axis=dim)
    leading = lax.slice_in_dim(array, 0, 1, axis=dim)
    before = lax.ppermute(last, axis, up)
    after = lax.ppermute(leading, axis, down)
    return jnp.concatenate([before, array, after], axis=dim)


def haloed(array):
    edged = padded(padded(array, "sx", 0), "sy", 2)
    return jnp.pad(edged, ((0, 0), (0, 0), (0, 0), (1, 1), (0, 0)))


def convolve(inputs, weights, layout):
    return lax.conv_general_dilated(
        inputs, weights, (1, 1, 1), ((0, 0),) * 3,
        dimension_numbers=layout, preferred_element_type=jnp.float32)


def local(features, kernel, filter_bias, cotangent):
    rows = kernel.shape[3] // lax.axis_size("sample")
    mine = lax.dynamic_slice_in_dim(kernel, lax.axis_index("sample") * rows, rows, axis=3)
    filts = kernel.shape[4]
    flat = mine.reshape(-1, filts)
    tail = jnp.broadcast_to(filter_bias[None], (16, filts))
    every = lax.all_gather(jnp.concatenate([flat, tail], axis=0), "sy", axis=0, tiled=False)
    bias = every[:, -1].reshape(-1)
    pieces = [every[n, :-16].reshape(mine.shape) for n in range(every.shape[0])]
    wide = jnp.concatenate(pieces, axis=4)
    full = lax.all_gather(wide, ("sx", "sample"), axis=3, tiled=True)
    cot = lax.all_to_all(cotangent, "sy", split_axis=2, concat_axis=4, tiled=True)
    window = haloed(features)
    hidden = convolve(window, full, ("DNHWC", "DHWIO", "DNHWC")) + bias.astype(jnp.float32)
    gate = jax.nn.sigmoid(hidden)
    output = (hidden * gate).astype(jnp.bfloat16)
    grad_pre = (cot.astype(jnp.float32) * (gate * (1.0 + hidden * (1.0 - gate)))).astype(jnp.bfloat16)
    output = lax.all_to_all(output, "sy", split_axis=4, concat_axis=2, tiled=True)
    local_grad = convolve(window, grad_pre, ("DCHWN", "DIHWO", "DHWNC")).astype(jnp.bfloat16)
    part = lax.psum_scatter(local_grad.astype(jnp.bfloat16), ("sx", "sample"), scatter_dimension=3, tiled=True)
    blocks = jnp.stack([part[..., n * filts:(n + 1) * filts] for n in range(lax.axis_size("sy"))])
    blocks = lax.all_to_all(blocks, "sy", split_axis=0, concat_axis=0, tiled=True)
    part = jnp.sum(blocks.astype(jnp.float32), axis=0).astype(jnp.bfloat16).reshape(mine.shape)
    kernel_grad = lax.all_gather(part, "sample", axis=3, tiled=True).astype(jnp.float32)
    input_grad = convolve(haloed(grad_pre), full[::-1, ::-1, ::-1], ("DNHWC", "DHWOI", "DNHWC")).astype(jnp.bfloat16)
    return output, input_grad, kernel_grad


def solution(mesh):
    return jax.shard_map(
        local, mesh=mesh,
        in_specs=(P("sx", "sample", "sy", None, None), P(None, None, None, "sx", "sy"),
                  P("sy"), P("sx", "sample", None, None, "sy")),
        out_specs=(P("sx", "sample", None, None, "sy"), P("sx", "sample", "sy", None, None),
                   P(None, None, None, "sx", "sy")),
        check_vma=False)
```

time: 272 us -> 172 us (0.63)
  waiting for transfers between devices: 132 us -> 26.3 us
  matrix products: 68.3 us -> 27.9 us
  starting transfers between devices: 11.7 us -> 35.5 us
  local copies, waits for them, and re-layouts: 18.4 us -> 39.9 us
    reduce_scatter x2 -> x1, waiting for transfers between devices: 62.9 us -> 10.5 us  [local(): lax.psum_scatter(local_grad.astype(jnp.bfloat16), ('sx', 'sample'), scatt...]
    all_gather x1, waiting for transfers between devices: 46.4 us -> 0.01 us  [local(): full = lax.all_gather(wide, ('sx', 'sample'), axis=3, tiled=True)]
    conv_general_dilated x3, matrix products: 68.3 us -> 27.9 us  [convolve(): lax.conv_general_dilated(inputs, weights, (1, 1, 1), ((0, 0),) * 3, dimen...]
    psum x1 -> x0, waiting for transfers between devices: 16.7 us -> none  [local(): kernel_grad = lax.psum(weight_sum, 'sample').astype(jnp.float32)]
    all_to_all x0 -> x3, starting transfers between devices: none -> 13.6 us  [the longest x1 5.38 us: local(): lax.all_to_all(cotangent, 'sy', split_axis=2, concat_axis=4, tiled=True)]
    unnamed x21 -> x33, local copies, waits for them, and re-layouts: 6.24 us -> 16.9 us
    ppermute x4 -> x8, starting transfers between devices: 11.5 us -> 21.9 us  [the longest x4 16.5 us: padded(): before = lax.ppermute(last, axis, up)]
    ppermute x4 -> x8, waiting for transfers between devices: 6.19 us -> 15.2 us  [the longest x4 7.79 us: padded(): before = lax.ppermute(last, axis, up)]
  transfers between devices with their start and end apart: 8 -> 13, of which waited for: 6 -> 6; matrix products, arithmetic and copies ran while one was open for 21% -> 27% of each run, Pallas kernels for 0% -> 0%
where the time goes in v1:
time: 172 us; the launch traced here: 171 us
  local copies, waits for them, and re-layouts  39.9 us (23%)
  starting transfers between devices  35.5 us (21%)
  matrix products  27.9 us (16%)
  waiting for transfers between devices  26.3 us (15%)
  blocking collectives  18.9 us (11%)
  between operations  14.4 us (8%)
  other arithmetic  8.49 us (5%)
    conv_general_dilated x3, matrix products, convolve(): lax.conv_general_dilated(inputs, weights, (1, 1, 1), ((0, 0),) * 3, dimen...  27.9 us
    unnamed x33, local copies, waits for them, and re-layouts  16.9 us
    all_gather x1, blocking collectives, local(): lax.all_gather(jnp.concatenate([flat, tail], axis=0), 'sy', axis=0, tiled...  16.8 us
    ppermute x4, starting transfers between devices, padded(): before = lax.ppermute(last, axis, up)  16.5 us
    reduce_scatter x1, waiting for transfers between devices, local(): lax.psum_scatter(local_grad.astype(jnp.bfloat16), ('sx', 'sample'), scatt...  10.5 us
    ppermute x4, waiting for transfers between devices, padded(): before = lax.ppermute(last, axis, up)  7.79 us
    ppermute x4, waiting for transfers between devices, padded(): after = lax.ppermute(leading, axis, down)  7.38 us
    concatenate x3, other arithmetic, padded(): return jnp.concatenate([before, array, after], axis=dim)  5.45 us
  transfers between devices with their start and end apart: 13, of which 6 were waited for; matrix products, arithmetic and copies ran while one was open for 27% of the time, Pallas kernels for 0%

profile of v1, /device:TPU:0, one launch (start us, length us, event | category | flops | bytes accessed | tf_op | source)
XLA Modules:
  0.0 171.4 jit_solution(12793810248107040166)
XLA Ops:
  9.1 16.8 %all-gather.1 = bf16[4,880,64]{1,2,0:T(8,128)(2,1)S(1)} all-gather(bf16[1,880,64]{1,2,0:T(8,128)(2,1)S(1)} %copy.93), channel_id=2, replica_groups=mesh['sample'=2,'sx'=4,'sy'=4] {'sy'}, dimensions={0}, use_global_device_ids=true | all-gather | bytes 563200 | tf_op jit(solution)/shard_map/all_gather | solution.py:35
  27.9 4.1 %collective-permute-start = (bf16[1,2,4,32,256]{4,1,3,2,0:T(2,128)(2,1)S(1)}, bf16[1,2,4,32,256]{4,1,3,2,0:T(2,128)(2,1)}, u32[]{:S(2)}, u32[]{:S(2)}) collective-permute-start(bf16[1,2,4,32,256]{4,1,3,2,0:T(2,128)(2,1)S(1)} %copy.116), channel_id=1, source_target_pairs={{0,4},{4,8},{8,12},{1,5},{5,9},{9,13},{2,6},{6,10},{10,14},{3,7},{... | collective-permute-start | bytes 393224 | tf_op jit(solution)/shard_map/ppermute | solution.py:13
  35.1 5.4 %all-to-all-start.1 = ((bf16[4,2,32768]{2,1,0:T(2,128)(2,1)}), bf16[4,2,32768]{2,1,0:T(2,128)(2,1)S(1)}, u32[]{:S(2)}, u32[]{:S(2)}) async-start(bf16[4,2,32768]{2,1,0:T(2,128)(2,1)} %reshape.55), calls=%async_computation.1 | async-start | bytes 1048576 | tf_op jit(solution)/shard_map/all_to_all | solution.py:40
  44.5 3.9 %collective-permute-start.2 = (bf16[6,2,1,32,256]{4,1,3,2,0:T(2,128)(2,1)S(1)}, bf16[6,2,1,32,256]{4,1,3,2,0:T(2,128)(2,1)S(1)}, u32[]{:S(2)}, u32[]{:S(2)}) collective-permute-start(bf16[6,2,1,32,256]{4,1,3,2,0:T(2,128)(2,1)S(1)} %get-tuple-element.22), channel_id=1, source_target_pairs={{0,1},{1,2},{2,3},{4,5},{5,6},{6,7},{8,9},{9,10},{10,11},{12,13},{... | collective-permute-start | bytes 589832 | tf_op jit(solution)/shard_map/ppermute | solution.py:13
  51.6 4.4 %collective-permute-done.3 = bf16[6,2,1,32,256]{4,1,3,2,0:T(2,128)(2,1)S(1)} collective-permute-done((bf16[6,2,1,32,256]{4,1,3,2,0:T(2,128)(2,1)S(1)}, bf16[6,2,1,32,256]{4,1,3,2,0:T(2,128)(2,1)S(1)}, u32[]{:S(2)}, u32[]{:S(2)}) %collective-permute-start.3) | collective-permute-done | bytes 196640 | tf_op jit(solution)/shard_map/ppermute | solution.py:14
  56.0 1.8 %fusion.39 = bf16[6,6,2,32,256]{4,2,3,1,0:T(2,128)(2,1)S(1)} fusion(bf16[6,2,1,32,256]{4,1,3,2,0:T(2,128)(2,1)S(1)} %collective-permute-done.3, bf16[6,2,4,32,256]{4,1,3,2,0:T(2,128)(2,1)S(1)} %constant_dynamic-update-slice_fusion, bf16[6,2,1,32,256]{4,1,3,2,0:T(2,128)(2,1)S(1)} %collective-permute-done.2), kind=kLoop, calls=%fused_computation.53 | loop fusion | flops 1179648 | bytes 2359296 | tf_op jit(solution)/shard_map/concatenate | solution.py:15
  62.9 2.0 %copy.119 = f32[4,2,4,4,32,64]{5,2,3,4,1,0:T(4,128)S(1)} copy(bf16[4,2,4,4,32,64]{5,4,1,0,3,2:T(8,128)(2,1)} %bitcast.76) | data formatting | bytes 1572864 | tf_op jit(solution)/shard_map/convert_element_type | solution.py:45
  65.0 2.3 %reshape.39 = f32[4,2,4,32,256]{4,2,3,1,0:T(4,128)} reshape(f32[4,2,4,32,4,64]{5,4,2,3,1,0:T(4,128)S(1)} %bitcast.72) | data formatting | bytes 2097152 | tf_op jit(solution)/shard_map/convert_element_type | solution.py:45
  67.3 8.8 %add_multiply_fusion = (f32[4,4,16,5,256]{4,2,3,1,0:T(8,128)S(1)}, bf16[4,4,16,5,256]{4,2,3,1,0:T(8,128)(2,1)}) fusion(f32[256]{0:T(256)S(1)} %reshape.38, bf16[3,3,3,256,256]{4,3,2,1,0:T(8,128)(2,1)} %all-gather.4.cloned.1.call-done, bf16[6,6,2,7,2,256]{5,3,2,4,1,0:T(8,128)(2,1)} %slice.77, bf16[6,6,2,8,5,256]{5,3,2,4,1,0:T(8,128)(2,1)} %copy-done.2, ...), kind=kOutput, calls=%fused_computation.22 | convolution fusion | flops 4539645952 | bytes 7496784 | tf_op jit(solution)/shard_map/conv_general_dilated | solution.py:24
  77.6 12.1 %convolution_convert_fusion = bf16[3,3,3,256,256]{4,3,2,1,0:T(8,128)(2,1)} fusion(bf16[4,2,4,32,256]{4,2,3,1,0:T(4,128)(2,1)S(1)} %fusion.29, bf16[6,2,1,32,256]{4,1,3,2,0:T(2,128)(2,1)S(1)} %copy-done.7, bf16[6,2,4,32,256]{4,1,3,2,0:T(2,128)(2,1)S(1)} %constant_dynamic-update-slice_fusion, bf16[6,2,1,32,256]{4,1,3,2,0:T(2,128)(2,1)S(1)} %collective-permute-done.2), kind=kOutput, calls=%fused_computation.3 | convolution fusion | flops 3553689600 | bytes 5242880 | tf_op jit(solution)/shard_map/conv_general_dilated | solution.py:24
  90.5 4.5 %collective-permute-start.4 = (bf16[1,2,4,32,256]{4,2,3,1,0:T(4,128)(2,1)}, bf16[1,2,4,32,256]{4,2,3,1,0:T(4,128)(2,1)S(1)}, u32[]{:S(2)}, u32[]{:S(2)}) collective-permute-start(bf16[1,2,4,32,256]{4,2,3,1,0:T(4,128)(2,1)} %get-tuple-element.24), channel_id=1, source_target_pairs={{0,4},{4,8},{8,12},{1,5},{5,9},{9,13},{2,6},{6,10},{10,14},{3,7},{... | collective-permute-start | bytes 393224 | tf_op jit(solution)/shard_map/ppermute | solution.py:13
  97.7 3.4 %copy.99 = bf16[4,2,4,32,256]{3,2,1,0,4:T(4,128)(2,1)S(1)} copy(bf16[4,2,4,32,256]{4,2,3,1,0:T(4,128)(2,1)} %slice_bitcast_fusion.2) | data formatting | bytes 1048576 | tf_op jit(solution)/shard_map/convert_element_type | solution.py:44
  101.1 2.9 %reshape.53 = bf16[4,2,32768]{2,1,0:T(2,128)(2,1)} reshape(bf16[256,4,2,4,32]{4,3,2,1,0:T(4,128)(2,1)S(1)} %bitcast.70) | data formatting | bytes 1048576
  104.1 3.6 %all-to-all-start = ((bf16[4,2,32768]{2,1,0:T(2,128)(2,1)}), bf16[4,2,32768]{2,1,0:T(2,128)(2,1)S(1)}, u32[]{:S(2)}, u32[]{:S(2)}) async-start(bf16[4,2,32768]{2,1,0:T(2,128)(2,1)} %reshape.53), calls=%async_computation | async-start | bytes 1048576 | tf_op jit(solution)/shard_map/all_to_all | solution.py:46
  110.0 3.9 %collective-permute-start.6 = (bf16[6,2,1,32,256]{4,2,3,1,0:T(2,128)(2,1)S(1)}, bf16[6,2,1,32,256]{4,2,3,1,0:T(2,128)(2,1)S(1)}, u32[]{:S(2)}, u32[]{:S(2)}) collective-permute-start(bf16[6,2,1,32,256]{4,2,3,1,0:T(2,128)(2,1)S(1)} %get-tuple-element.20), channel_id=1, source_target_pairs={{0,1},{1,2},{2,3},{4,5},{5,6},{6,7},{8,9},{9,10},{10,11},{12,13},{... | collective-permute-start | bytes 589832 | tf_op jit(solution)/shard_map/ppermute | solution.py:13
  115.3 6.4 %collective-permute-done.6 = bf16[6,2,1,32,256]{4,2,3,1,0:T(2,128)(2,1)S(1)} collective-permute-done((bf16[6,2,1,32,256]{4,2,3,1,0:T(2,128)(2,1)S(1)}, bf16[6,2,1,32,256]{4,2,3,1,0:T(2,128)(2,1)S(1)}, u32[]{:S(2)}, u32[]{:S(2)}) %collective-permute-start.6) | collective-permute-done | bytes 196640 | tf_op jit(solution)/shard_map/ppermute | solution.py:13
  121.6 3.0 %collective-permute-done.7 = bf16[6,2,1,32,256]{4,2,3,1,0:T(2,128)(2,1)S(1)} collective-permute-done((bf16[6,2,1,32,256]{4,2,3,1,0:T(2,128)(2,1)S(1)}, bf16[6,2,1,32,256]{4,2,3,1,0:T(2,128)(2,1)S(1)}, u32[]{:S(2)}, u32[]{:S(2)}) %collective-permute-start.7) | collective-permute-done | bytes 196640 | tf_op jit(solution)/shard_map/ppermute | solution.py:14
  124.6 2.2 %maximum_bitcast_fusion = bf16[6,6,2,32,256]{4,1,3,2,0:T(8,128)(2,1)S(1)} fusion(bf16[6,2,1,32,256]{4,2,3,1,0:T(2,128)(2,1)S(1)} %collective-permute-done.7, bf16[1,2,4,32,256]{4,2,3,1,0:T(4,128)(2,1)} %collective-permute-done.5, bf16[4,2,4,32,256]{4,2,3,1,0:T(4,128)(2,1)S(1)} %fusion.29, bf16[1,2,4,32,256]{4,2,3,1,0:T(4,128)(2,1)S(1)} %collective-permute-done.4, ...), kind=kLoop, calls=%fused_computation.17 | loop fusion | flops 5898240 | bytes 2359296 | tf_op jit(solution)/shard_map/concatenate | solution.py:15
  128.4 10.5 %reduce-scatter.2.cloned.1.call-done = bf16[3,3,3,32,256]{4,3,2,1,0:T(8,128)(2,1)} async-done(((bf16[3,3,3,256,256]{4,3,2,1,0:T(8,128)(2,1)}), bf16[3,3,3,32,256]{4,3,2,1,0:T(8,128)(2,1)}) %reduce-scatter.2.cloned.1.call-update) | async-done | bytes 442384 | tf_op jit(solution)/shard_map/reduce_scatter | solution.py:48
  141.9 4.6 %all-to-all-start.2 = ((bf16[4,2,27648]{2,1,0:T(2,128)(2,1)}), bf16[4,2,27648]{2,1,0:T(2,128)(2,1)}, u32[]{:S(2)}, u32[]{:S(2)}) async-start(bf16[4,2,27648]{2,1,0:T(2,128)(2,1)} %reshape.57), calls=%async_computation.3 | async-start | bytes 884736 | tf_op jit(solution)/shard_map/all_to_all | solution.py:50
  146.5 7.0 %fusion.25 = bf16[4,4,16,5,256]{4,2,3,1,0:T(8,128)(2,1)S(1)} fusion(bf16[3,3,3,256,256]{4,3,2,1,0:T(8,128)(2,1)} %all-gather.4.cloned.1.call-done, bf16[6,6,2,7,2,256]{5,3,2,4,1,0:T(8,128)(2,1)} %slice.89, bf16[6,6,2,8,5,256]{5,3,2,4,1,0:T(8,128)(2,1)S(1)} %copy.106, pred[16,5]{0,1:T(8,128)(4,1)S(1)} %copy-done.9), kind=kOutput, calls=%fused_computation.21 | convolution fusion | flops 4536696832 | bytes 6185040 | tf_op jit(solution)/shard_map/conv_general_dilated | solution.py:24
  156.0 2.5 %copy.101 = bf16[4,2,4,4,32,64]{5,4,3,2,1,0:T(8,128)(2,1)} copy(bf16[4,2,4,4,32,64]{4,3,1,0,5,2:T(4,128)(2,1)S(1)} %bitcast.71) | data formatting | bytes 1048576 | tf_op jit(solution)/shard_map/all_to_all | solution.py:46
  159.2 2.0 %reshape.58 = bf16[4,3,3,3,32,64]{5,4,3,2,1,0:T(8,128)(2,1)S(1)} reshape(bf16[4,2,27648]{2,1,0:T(2,128)(2,1)} %all-to-all-done.2) | data formatting | bytes 884736
  161.4 2.1 %all_gather.15 = bf16[3,3,3,64,64]{4,3,2,1,0:T(8,128)(2,1)S(1)} all-gather(bf16[3,3,3,32,64]{4,3,2,1,0:T(8,128)(2,1)S(1)} %reduce_sum.12), channel_id=1, replica_groups=mesh['sample'=2,'sx'=4,'sy'=4] {'sample'}, dimensions={3}, use_global_device_ids=true | all-gather | bytes 331776 | tf_op jit(solution)/shard_map/all_gather | solution.py:52
  (81 shorter events, 36.7 us)
Async XLA Ops:
  7.2 1.0 copy-start
  7.2 60.1 %all-gather.4.cloned.1.call-start = ((), (), s32[]{:S(2)}) async-start(), calls=%async_computation.4 | async-start | bytes 3981312 | tf_op jit(solution)/shard_map/all_gather | solution.py:39
  25.8 1.9 %copy-start.3 = (bf16[4,2,4,32,256]{4,3,2,1,0:T(8,128)(2,1)S(1)}, bf16[4,2,4,32,256]{4,3,2,1,0:T(8,128)(2,1)}, u32[]{:S(2)}) copy-start(bf16[4,2,4,32,256]{4,3,2,1,0:T(8,128)(2,1)} %param.4) | copy-start | bytes 1572868
  25.9 7.5 %copy-start.4 = (bf16[4,2,16,32,64]{4,3,2,1,0:T(8,128)(2,1)S(1)}, bf16[4,2,16,32,64]{4,3,2,1,0:T(8,128)(2,1)}, u32[]{:S(2)}) copy-start(bf16[4,2,16,32,64]{4,3,2,1,0:T(8,128)(2,1)} %param.7) | copy-start | bytes 1572868
  27.9 12.6 %collective-permute-start = (bf16[1,2,4,32,256]{4,1,3,2,0:T(2,128)(2,1)S(1)}, bf16[1,2,4,32,256]{4,1,3,2,0:T(2,128)(2,1)}, u32[]{:S(2)}, u32[]{:S(2)}) collective-permute-start(bf16[1,2,4,32,256]{4,1,3,2,0:T(2,128)(2,1)S(1)} %copy.116), channel_id=1, source_target_pairs={{0,4},{4,8},{8,12},{1,5},{5,9},{9,13},{2,6},{6,10},{10,14},{3,7},{... | collective-permute-start | bytes 393224 | tf_op jit(solution)/shard_map/ppermute | solution.py:13
  32.1 11.0 %collective-permute-start.1 = (bf16[1,2,4,32,256]{4,1,3,2,0:T(2,128)(2,1)S(1)}, bf16[1,2,4,32,256]{4,1,3,2,0:T(2,128)(2,1)}, u32[]{:S(2)}, u32[]{:S(2)}) collective-permute-start(bf16[1,2,4,32,256]{4,1,3,2,0:T(2,128)(2,1)S(1)} %copy.117), channel_id=1, source_target_pairs={{4,0},{8,4},{12,8},{5,1},{9,5},{13,9},{6,2},{10,6},{14,10},{7,3},{... | collective-permute-start | bytes 393224 | tf_op jit(solution)/shard_map/ppermute | solution.py:14
  35.1 26.3 %all-to-all-start.1 = ((bf16[4,2,32768]{2,1,0:T(2,128)(2,1)}), bf16[4,2,32768]{2,1,0:T(2,128)(2,1)S(1)}, u32[]{:S(2)}, u32[]{:S(2)}) async-start(bf16[4,2,32768]{2,1,0:T(2,128)(2,1)} %reshape.55), calls=%async_computation.1 | async-start | bytes 1048576 | tf_op jit(solution)/shard_map/all_to_all | solution.py:40
  40.5 98.4 %reduce-scatter.2.cloned.1.call-start = ((), (), s32[]{:S(2)}) async-start(), calls=%async_computation.5 | async-start | bytes 3981312 | tf_op jit(solution)/shard_map/reduce_scatter | solution.py:48
  44.5 7.1 %collective-permute-start.2 = (bf16[6,2,1,32,256]{4,1,3,2,0:T(2,128)(2,1)S(1)}, bf16[6,2,1,32,256]{4,1,3,2,0:T(2,128)(2,1)S(1)}, u32[]{:S(2)}, u32[]{:S(2)}) collective-permute-start(bf16[6,2,1,32,256]{4,1,3,2,0:T(2,128)(2,1)S(1)} %get-tuple-element.22), channel_id=1, source_target_pairs={{0,1},{1,2},{2,3},{4,5},{5,6},{6,7},{8,9},{9,10},{10,11},{12,13},{... | collective-permute-start | bytes 589832 | tf_op jit(solution)/shard_map/ppermute | solution.py:13
  48.4 7.6 %collective-permute-start.3 = (bf16[6,2,1,32,256]{4,1,3,2,0:T(2,128)(2,1)S(1)}, bf16[6,2,1,32,256]{4,1,3,2,0:T(2,128)(2,1)S(1)}, u32[]{:S(2)}, u32[]{:S(2)}) collective-permute-start(bf16[6,2,1,32,256]{4,1,3,2,0:T(2,128)(2,1)S(1)} %get-tuple-element.23), channel_id=1, source_target_pairs={{1,0},{2,1},{3,2},{5,4},{6,5},{7,6},{9,8},{10,9},{11,10},{13,12},{... | collective-permute-start | bytes 589832 | tf_op jit(solution)/shard_map/ppermute | solution.py:14
  56.0 3.0 %copy-start.6 = (bf16[6,2,1,32,256]{4,1,3,2,0:T(2,128)(2,1)}, bf16[6,2,1,32,256]{4,1,3,2,0:T(2,128)(2,1)S(1)}, u32[]{:S(2)}) copy-start(bf16[6,2,1,32,256]{4,1,3,2,0:T(2,128)(2,1)S(1)} %collective-permute-done.3) | copy-start | bytes 589828
  59.3 1.1 copy-start.2
  65.0 2.3 %copy-start.8 = (pred[16,5]{0,1:T(8,128)(4,1)S(1)}, pred[16,5]{0,1:T(8,128)(4,1)}, u32[]{:S(2)}) copy-start(pred[16,5]{0,1:T(8,128)(4,1)} %constant.26) | copy-start | bytes 244
  76.1 1.2 copy-start.1
  76.1 1.5 copy-start.7
  89.7 6.7 %copy-start.5 = (bf16[4,4,16,5,256]{4,2,3,1,0:T(8,128)(2,1)S(1)}, bf16[4,4,16,5,256]{4,2,3,1,0:T(8,128)(2,1)}, u32[]{:S(2)}) copy-start(bf16[4,4,16,5,256]{4,2,3,1,0:T(8,128)(2,1)} %get-tuple-element.19) | copy-start | bytes 1966084
  90.5 17.2 %collective-permute-start.4 = (bf16[1,2,4,32,256]{4,2,3,1,0:T(4,128)(2,1)}, bf16[1,2,4,32,256]{4,2,3,1,0:T(4,128)(2,1)S(1)}, u32[]{:S(2)}, u32[]{:S(2)}) collective-permute-start(bf16[1,2,4,32,256]{4,2,3,1,0:T(4,128)(2,1)} %get-tuple-element.24), channel_id=1, source_target_pairs={{0,4},{4,8},{8,12},{1,5},{5,9},{9,13},{2,6},{6,10},{10,14},{3,7},{... | collective-permute-start | bytes 393224 | tf_op jit(solution)/shard_map/ppermute | solution.py:13
  95.1 12.6 %collective-permute-start.5 = (bf16[1,2,4,32,256]{4,2,3,1,0:T(4,128)(2,1)}, bf16[1,2,4,32,256]{4,2,3,1,0:T(4,128)(2,1)}, u32[]{:S(2)}, u32[]{:S(2)}) collective-permute-start(bf16[1,2,4,32,256]{4,2,3,1,0:T(4,128)(2,1)} %get-tuple-element.25), channel_id=1, source_target_pairs={{4,0},{8,4},{12,8},{5,1},{9,5},{13,9},{6,2},{10,6},{14,10},{7,3},{... | collective-permute-start | bytes 393224 | tf_op jit(solution)/shard_map/ppermute | solution.py:14
  104.1 37.8 %all-to-all-start = ((bf16[4,2,32768]{2,1,0:T(2,128)(2,1)}), bf16[4,2,32768]{2,1,0:T(2,128)(2,1)S(1)}, u32[]{:S(2)}, u32[]{:S(2)}) async-start(bf16[4,2,32768]{2,1,0:T(2,128)(2,1)} %reshape.53), calls=%async_computation | async-start | bytes 1048576 | tf_op jit(solution)/shard_map/all_to_all | solution.py:46
  110.0 11.6 %collective-permute-start.6 = (bf16[6,2,1,32,256]{4,2,3,1,0:T(2,128)(2,1)S(1)}, bf16[6,2,1,32,256]{4,2,3,1,0:T(2,128)(2,1)S(1)}, u32[]{:S(2)}, u32[]{:S(2)}) collective-permute-start(bf16[6,2,1,32,256]{4,2,3,1,0:T(2,128)(2,1)S(1)} %get-tuple-element.20), channel_id=1, source_target_pairs={{0,1},{1,2},{2,3},{4,5},{5,6},{6,7},{8,9},{9,10},{10,11},{12,13},{... | collective-permute-start | bytes 589832 | tf_op jit(solution)/shard_map/ppermute | solution.py:13
  114.0 10.6 %collective-permute-start.7 = (bf16[6,2,1,32,256]{4,2,3,1,0:T(2,128)(2,1)S(1)}, bf16[6,2,1,32,256]{4,2,3,1,0:T(2,128)(2,1)S(1)}, u32[]{:S(2)}, u32[]{:S(2)}) collective-permute-start(bf16[6,2,1,32,256]{4,2,3,1,0:T(2,128)(2,1)S(1)} %get-tuple-element.21), channel_id=1, source_target_pairs={{1,0},{2,1},{3,2},{5,4},{6,5},{7,6},{9,8},{10,9},{11,10},{13,12},{... | collective-permute-start | bytes 589832 | tf_op jit(solution)/shard_map/ppermute | solution.py:14
  140.3 6.2 %copy-start.9 = (pred[16,5]{0,1:T(8,128)(4,1)S(1)}, pred[16,5]{0,1:T(8,128)(4,1)}, u32[]{:S(2)}) copy-start(pred[16,5]{0,1:T(8,128)(4,1)} %constant.26) | copy-start | bytes 244
  141.9 17.3 %all-to-all-start.2 = ((bf16[4,2,27648]{2,1,0:T(2,128)(2,1)}), bf16[4,2,27648]{2,1,0:T(2,128)(2,1)}, u32[]{:S(2)}, u32[]{:S(2)}) async-start(bf16[4,2,27648]{2,1,0:T(2,128)(2,1)} %reshape.57), calls=%async_computation.3 | async-start | bytes 884736 | tf_op jit(solution)/shard_map/all_to_all | solution.py:50
Sparse Core Ops, SparseCore 0:
  27.8 35.7 all-gather.3
  89.9 48.9 reduce-scatter.1
